TPU v7x, 32 devices: a whole 2x2x4 slice. The times are simulated.
32 devices in a mesh: wide: 8 (over z, x), narrow: 4 (over y, core).
Axes of the slice: x: 2, y: 2, z: 4, core: 2. Of those that a mesh axis runs over, the one named last changes fastest.
Arguments:
- tokens: bfloat16 [16384, 768], P(('wide', 'narrow')), may hold values from -6 to 6
- timestep: int32 [16], P('wide'), may hold values from 0 to 999
- token_mask: int32 [16384], P(('wide', 'narrow')), may hold values 0 or 1
- time_table: float32 [1000, 128], replicated, may hold values from -6 to 6
- w_ada: bfloat16 [128, 4608], replicated, may hold values from -0.5 to 0.5
- b_ada: float32 [4608], replicated, may hold values from -3 to 3
- gain_one: float32 [768], replicated, may hold values from 0.5 to 1.5
- w_qkv: bfloat16 [3, 768, 768], P(None, None, 'narrow'), may hold values from -0.21875 to 0.21875
- w_out: bfloat16 [768, 768], P('narrow'), may hold values from -3.5 to 3.5
- gain_two: float32 [768], replicated, may hold values from 0.5 to 1.5
- w_up: bfloat16 [768, 3072], P(None, 'narrow'), may hold values from -0.21875 to 0.21875
- b_up: float32 [3072], P('narrow'), may hold values from -3 to 3
- w_down: bfloat16 [3072, 768], P('narrow'), may hold values from -0.109375 to 0.109375
- b_down: float32 [768], replicated, may hold values from -3 to 3
- cotangent: bfloat16 [16384, 768], P(('wide', 'narrow')), may hold values from -6 to 6
Outputs:
- mixed: bfloat16 [16384, 768], P(('wide', 'narrow'))
- grad_tokens: float32 [16384, 768], P(('wide', 'narrow'))
- grad_time_table: float32 [1000, 128], replicated
- grad_w_ada: float32 [128, 4608], replicated
- grad_b_ada: float32 [4608], replicated
- grad_gain_one: float32 [768], replicated
- grad_w_qkv: float32 [3, 768, 768], P(None, None, 'narrow')
- grad_w_out: float32 [768, 768], P('narrow')
- grad_gain_two: float32 [768], replicated
- grad_w_up: float32 [768, 3072], P(None, 'narrow')
- grad_b_up: float32 [3072], P('narrow')
- grad_w_down: float32 [3072, 768], P('narrow')
- grad_b_down: float32 [768], replicated
Inputs may be any that keep to these rules, and one draw needn't show every extreme that they name: One timestep for each sequence of 1024 tokens.
All inputs are finite; a program needn't handle non-finite values. No bound on the sum of `token_mask` on one device may be relied on, other than what follows from the above.
Results may differ from a plain program's by a relative error of at most 0.02.
The roundings to bfloat16 on the way count: a program that leaves them out, or rounds other values in their place, can miss the bound.
Values may be sent and summed in bfloat16 or wider, within the bound.
A program may use at most 192 MiB of HBM per device.

v0:
```python
from functools import partial
import math
import jax
import jax.numpy as jnp
from jax import lax
from jax.sharding import PartitionSpec as P

D = 768
HD = 64
LEN = 1024
SEQS = 2
norm_eps = 1e-06
highest = lax.Precision.HIGHEST


def layer_norm(values, norm_gain):
    centered = values - jnp.mean(values, axis=-1, keepdims=True)
    variance = jnp.mean(centered * centered, axis=-1, keepdims=True)
    return centered * lax.rsqrt(variance + norm_eps) * norm_gain


def norm_back(values, norm_gain, grad_norm):
    _, pullback = jax.vjp(layer_norm, values, norm_gain)
    return pullback(grad_norm)


def rope_tables():
    half_width = HD // 2
    frequency = 10000.0 ** (-2.0 * jnp.arange(half_width, dtype=jnp.float32) / HD)
    angles = jnp.arange(LEN, dtype=jnp.float32)[:, None] * frequency[None, :]
    cos_table = jnp.concatenate([jnp.cos(angles), jnp.cos(angles)], axis=1)[:, None, :]
    sin_table = jnp.concatenate([jnp.sin(angles), jnp.sin(angles)], axis=1)[:, None, :]
    return (cos_table, sin_table)


def rotate(values, cos_table, sin_table):
    half_width = values.shape[-1] // 2
    turned = jnp.concatenate([-values[..., half_width:], values[..., :half_width]], axis=-1)
    return values * cos_table + turned * sin_table


def attend(q_low, k_low, v_low):
    scale_factor = 1.0 / math.sqrt(HD)
    block_rows = min(512, LEN)

    def one_sequence(pieces):
        q_seq, k_seq, v_seq = pieces
        outputs = []
        log_parts = []
        for first_row in range(0, LEN, block_rows):
            scores = (
                jnp.einsum(
                    "qhe,khe->hqk",
                    q_seq[first_row : first_row + block_rows],
                    k_seq,
                    preferred_element_type=jnp.float32,
                )
                * scale_factor
            )
            row_max = jnp.max(scores, axis=-1, keepdims=True)
            exp_scores = jnp.exp(scores - row_max)
            row_sum = jnp.sum(exp_scores, axis=-1, keepdims=True)
            probs_low = (exp_scores / row_sum).astype(jnp.bfloat16)
            outputs.append(
                jnp.einsum("hqk,khe->qhe", probs_low, v_seq, preferred_element_type=jnp.float32)
            )
            log_parts.append((row_max + jnp.log(row_sum))[..., 0])
        return (jnp.concatenate(outputs, axis=0), jnp.concatenate(log_parts, axis=1))

    return lax.map(one_sequence, (q_low, k_low, v_low))


def attend_back(q_low, k_low, v_low, log_sums, grad_heads):
    scale_factor = 1.0 / math.sqrt(HD)
    block_rows = min(512, LEN)

    def one_sequence(pieces):
        q_seq, k_seq, v_seq, sums_seq, grad_seq = pieces
        grad_keys = jnp.zeros(k_seq.shape, jnp.float32)
        grad_values = jnp.zeros(v_seq.shape, jnp.float32)
        grad_queries = []
        for first_row in range(0, LEN, block_rows):
            q_block = q_seq[first_row : first_row + block_rows]
            grad_block = grad_seq[first_row : first_row + block_rows]
            scores = (
                jnp.einsum("qhe,khe->hqk", q_block, k_seq, preferred_element_type=jnp.float32)
                * scale_factor
            )
            probs = jnp.exp(scores - sums_seq[:, first_row : first_row + block_rows, None])
            probs_low = probs.astype(jnp.bfloat16)
            grad_values = grad_values + jnp.einsum(
                "hqk,qhe->khe", probs_low, grad_block, preferred_element_type=jnp.float32
            )
            grad_probs = jnp.einsum(
                "qhe,khe->hqk", grad_block, v_seq, preferred_element_type=jnp.float32
            )
            inner_sum = jnp.sum(probs * grad_probs, axis=-1, keepdims=True)
            grad_scores = (probs * (grad_probs - inner_sum) * scale_factor).astype(jnp.bfloat16)
            grad_queries.append(
                jnp.einsum("hqk,khe->qhe", grad_scores, k_seq, preferred_element_type=jnp.float32)
            )
            grad_keys = grad_keys + jnp.einsum(
                "hqk,qhe->khe", grad_scores, q_block, preferred_element_type=jnp.float32
            )
        return (jnp.concatenate(grad_queries, axis=0), grad_keys, grad_values)

    return lax.map(one_sequence, (q_low, k_low, v_low, log_sums, grad_heads))


def forward(
    tokens,
    timestep,
    time_table,
    w_ada,
    b_ada,
    gain_one,
    w_qkv,
    w_out,
    gain_two,
    w_up,
    b_up,
    w_down,
    b_down,
):
    tok_rows = tokens.shape[0]
    group_heads = w_qkv.shape[2] // HD
    step_pick = (
        timestep[:, None] == jnp.arange(time_table.shape[0], dtype=jnp.int32)[None, :]
    ).astype(jnp.float32)
    picked = jnp.dot(step_pick, time_table, precision=highest)
    cond_low = jax.nn.silu(picked).astype(jnp.bfloat16)
    modulation = jnp.dot(cond_low, w_ada, preferred_element_type=jnp.float32) + b_ada
    positions = lax.axis_index("narrow") * tok_rows + jnp.arange(tok_rows, dtype=jnp.int32)
    row_pick = (positions[:, None] // LEN == jnp.arange(SEQS, dtype=jnp.int32)[None, :]).astype(
        jnp.float32
    )
    mod_tok = jnp.dot(row_pick, modulation, precision=highest).reshape(tok_rows, 6, D)
    residual_in = tokens.astype(jnp.float32)
    norm_one = layer_norm(residual_in, gain_one)
    normed_low = (norm_one * (1.0 + mod_tok[:, 1]) + mod_tok[:, 0]).astype(jnp.bfloat16)
    normed_all = lax.all_gather(normed_low, "narrow", axis=0, tiled=True)
    projected = jnp.einsum("td,kde->kte", normed_all, w_qkv, preferred_element_type=jnp.float32)
    shaped = projected.reshape(3, SEQS, LEN, group_heads, HD)
    cos_table, sin_table = rope_tables()
    q_low = rotate(shaped[0], cos_table, sin_table).astype(jnp.bfloat16)
    k_low = rotate(shaped[1], cos_table, sin_table).astype(jnp.bfloat16)
    v_low = shaped[2].astype(jnp.bfloat16)
    head_out, log_sums = attend(q_low, k_low, v_low)
    heads_low = head_out.astype(jnp.bfloat16).reshape(SEQS * LEN, group_heads * HD)
    attn_part = lax.psum_scatter(
        jnp.dot(
            lax.slice_in_dim(heads_low, 0, tok_rows * lax.axis_size("narrow"), axis=0),
            w_out,
            preferred_element_type=jnp.float32,
        ).astype(jnp.bfloat16),
        "narrow",
        scatter_dimension=0,
        tiled=True,
    ).astype(jnp.float32)
    mid_residual = residual_in + mod_tok[:, 2] * attn_part
    norm_two = layer_norm(mid_residual, gain_two)
    normed_two_low = (norm_two * (1.0 + mod_tok[:, 4]) + mod_tok[:, 3]).astype(jnp.bfloat16)
    normed_two_all = lax.all_gather(normed_two_low, "narrow", axis=0, tiled=True)
    pre_act = jnp.dot(normed_two_all, w_up, preferred_element_type=jnp.float32) + b_up
    act_low = jax.nn.gelu(pre_act, approximate=True).astype(jnp.bfloat16)
    branch = (
        lax.psum_scatter(
            jnp.dot(
                lax.slice_in_dim(act_low, 0, tok_rows * lax.axis_size("narrow"), axis=0),
                w_down,
                preferred_element_type=jnp.float32,
            ).astype(jnp.bfloat16),
            "narrow",
            scatter_dimension=0,
            tiled=True,
        ).astype(jnp.float32)
        + b_down
    )
    mixed = mid_residual + mod_tok[:, 5] * branch
    return (
        mixed,
        step_pick,
        picked,
        cond_low,
        row_pick,
        mod_tok,
        residual_in,
        norm_one,
        normed_all,
        q_low,
        k_low,
        v_low,
        log_sums,
        heads_low,
        attn_part,
        mid_residual,
        norm_two,
        normed_two_all,
        pre_act,
        act_low,
        branch,
    )


def body(
    tokens,
    timestep,
    token_mask,
    time_table,
    w_ada,
    b_ada,
    gain_one,
    w_qkv,
    w_out,
    gain_two,
    w_up,
    b_up,
    w_down,
    b_down,
    cotangent,
):
    weights = (
        time_table,
        w_ada,
        b_ada,
        gain_one,
        w_qkv,
        w_out,
        gain_two,
        w_up,
        b_up,
        w_down,
        b_down,
    )
    saved = forward(tokens, timestep, *weights)
    (
        mixed,
        step_pick,
        picked,
        cond_low,
        row_pick,
        mod_tok,
        residual_in,
        norm_one,
        normed_all,
        q_low,
        k_low,
        v_low,
        log_sums,
        heads_low,
        attn_part,
        mid_residual,
        norm_two,
        normed_two_all,
        pre_act,
        act_low,
        branch,
    ) = saved
    tok_rows = tokens.shape[0]
    group_heads = w_qkv.shape[2] // HD
    grad_mixed = cotangent.astype(jnp.float32) * token_mask.astype(jnp.float32)[:, None]
    grad_gate_two = grad_mixed * branch
    grad_branch = grad_mixed * mod_tok[:, 5]
    b_down_part = jnp.sum(grad_branch, axis=0)
    branch_all = lax.all_gather(grad_branch.astype(jnp.bfloat16), "narrow", axis=0, tiled=True)
    grad_w_down = jnp.einsum("tf,td->fd", act_low, branch_all, preferred_element_type=jnp.float32)
    grad_act = jnp.einsum("td,fd->tf", branch_all, w_down, preferred_element_type=jnp.float32)
    _, gelu_pull = jax.vjp(partial(jax.nn.gelu, approximate=True), pre_act)
    grad_pre_low = gelu_pull(grad_act)[0].astype(jnp.bfloat16)
    grad_b_up = jnp.sum(grad_pre_low, axis=0, dtype=jnp.float32)
    grad_w_up = jnp.einsum(
        "td,tf->df", normed_two_all, grad_pre_low, preferred_element_type=jnp.float32
    )
    grad_normed_two = lax.psum_scatter(
        jnp.einsum(
            "tf,df->td",
            lax.slice_in_dim(grad_pre_low, 0, tok_rows * lax.axis_size("narrow"), axis=0),
            w_up,
            preferred_element_type=jnp.float32,
        ).astype(jnp.bfloat16),
        "narrow",
        scatter_dimension=0,
        tiled=True,
    ).astype(jnp.float32)
    grad_res_two, gain_two_part = norm_back(
        mid_residual, gain_two, grad_normed_two * (1.0 + mod_tok[:, 4])
    )
    grad_mid = grad_mixed + grad_res_two
    grad_gate_one = grad_mid * attn_part
    attention_all = lax.all_gather(
        (grad_mid * mod_tok[:, 2]).astype(jnp.bfloat16), "narrow", axis=0, tiled=True
    )
    grad_w_out = jnp.einsum(
        "te,td->ed", heads_low, attention_all, preferred_element_type=jnp.float32
    )
    grad_heads = jnp.einsum("td,ed->te", attention_all, w_out, preferred_element_type=jnp.float32)
    grad_heads = grad_heads.astype(jnp.bfloat16).reshape(SEQS, LEN, group_heads, HD)
    grad_queries, grad_keys, grad_values = attend_back(q_low, k_low, v_low, log_sums, grad_heads)
    cos_table, sin_table = rope_tables()
    _, rope_pull = jax.vjp(lambda values: rotate(values, cos_table, sin_table), grad_queries)
    grad_projected = jnp.stack([rope_pull(grad_queries)[0], rope_pull(grad_keys)[0], grad_values])
    grad_projected = grad_projected.reshape(3, SEQS * LEN, group_heads * HD).astype(jnp.bfloat16)
    grad_w_qkv = jnp.einsum(
        "td,kte->kde", normed_all, grad_projected, preferred_element_type=jnp.float32
    )
    grad_normed = lax.psum_scatter(
        jnp.einsum("kte,kde->td", grad_projected, w_qkv, preferred_element_type=jnp.float32).astype(
            jnp.bfloat16
        ),
        "narrow",
        scatter_dimension=0,
        tiled=True,
    ).astype(jnp.float32)
    grad_res_one, gain_one_part = norm_back(
        residual_in, gain_one, grad_normed * (1.0 + mod_tok[:, 1])
    )
    grad_tokens = grad_mid + grad_res_one
    grad_mod_flat = jnp.stack(
        [
            grad_normed,
            grad_normed * norm_one,
            grad_gate_one,
            grad_normed_two,
            grad_normed_two * norm_two,
            grad_gate_two,
        ],
        axis=1,
    ).reshape(tok_rows, 6 * D)
    mod_part = jnp.einsum("ts,tm->sm", row_pick, grad_mod_flat, precision=highest)
    grad_modulation, grad_gain_one, grad_gain_two, grad_b_down = (
        lax.psum(mod_part.astype(jnp.bfloat16), "narrow").astype(jnp.float32),
        lax.psum(gain_one_part.astype(jnp.bfloat16), "narrow").astype(jnp.float32),
        lax.psum(gain_two_part.astype(jnp.bfloat16), "narrow").astype(jnp.float32),
        lax.psum(b_down_part.astype(jnp.bfloat16), "narrow").astype(jnp.float32),
    )
    all_modulation = lax.all_gather(grad_modulation, "wide", axis=0, tiled=True)
    all_steps = lax.all_gather(timestep, "wide", axis=0, tiled=True)
    all_pick = (
        all_steps[:, None] == jnp.arange(time_table.shape[0], dtype=jnp.int32)[None, :]
    ).astype(jnp.float32)
    all_picked = jnp.dot(all_pick, time_table, precision=highest)
    all_cond = jax.nn.silu(all_picked).astype(jnp.bfloat16)
    grad_b_ada = jnp.sum(all_modulation, axis=0)
    modulation_low = all_modulation.astype(jnp.bfloat16)
    grad_w_ada = jnp.einsum(
        "sc,sm->cm", all_cond, modulation_low, preferred_element_type=jnp.float32
    )
    grad_condition = jnp.einsum(
        "sm,cm->sc", modulation_low, w_ada, preferred_element_type=jnp.float32
    )
    _, silu_pull = jax.vjp(jax.nn.silu, all_picked)
    grad_time_table = jnp.einsum(
        "sn,sc->nc", all_pick, silu_pull(grad_condition)[0], precision=highest
    )

    def reduce_low(values):
        return lax.psum(values.astype(jnp.bfloat16), "wide").astype(jnp.float32)

    grad_gain_one = reduce_low(grad_gain_one)
    grad_gain_two = reduce_low(grad_gain_two)
    grad_b_up = reduce_low(grad_b_up)
    grad_b_down = reduce_low(grad_b_down)
    grad_w_qkv = reduce_low(grad_w_qkv)
    grad_w_out = reduce_low(grad_w_out)
    grad_w_up = reduce_low(grad_w_up)
    grad_w_down = reduce_low(grad_w_down)
    return (
        mixed.astype(jnp.bfloat16),
        grad_tokens,
        grad_time_table,
        grad_w_ada,
        grad_b_ada,
        grad_gain_one,
        grad_w_qkv,
        grad_w_out,
        grad_gain_two,
        grad_w_up,
        grad_b_up,
        grad_w_down,
        grad_b_down,
    )


def solution(mesh):
    return jax.shard_map(
        body,
        mesh=mesh,
        in_specs=(
            P(("wide", "narrow"), None),
            P("wide"),
            P(("wide", "narrow")),
            P(),
            P(),
            P(),
            P(),
            P(None, None, "narrow"),
            P("narrow", None),
            P(),
            P(None, "narrow"),
            P("narrow"),
            P("narrow", None),
            P(),
            P(("wide", "narrow"), None),
        ),
        out_specs=(
            P(("wide", "narrow"), None),
            P(("wide", "narrow"), None),
            P(),
            P(),
            P(),
            P(),
            P(None, None, "narrow"),
            P("narrow", None),
            P(),
            P(None, "narrow"),
            P("narrow"),
            P("narrow", None),
            P(),
        ),
        check_vma=False,
    )
```

profile of v0, /device:TPU:0, one launch (start us, length us, event | category | flops | bytes accessed | tf_op | source)
XLA Modules:
  0.0 828.8 jit_solution(5324140804440143015)
XLA Ops:
  32.8 27.8 %all-gather.6.cloned.1.call-done = bf16[2048,768]{1,0:T(8,128)(2,1)} async-done(((bf16[512,768]{1,0:T(8,128)(2,1)}), bf16[2048,768]{1,0:T(8,128)(2,1)}) %all-gather.6.cloned.1.call-update) | async-done | bytes 3145744 | tf_op jit(solution)/shard_map/all_gather | solution.py:141
  81.2 20.5 %while.28 = (s32[]{:T(128)}, bf16[2,1024,3,64]{1,3,2,0:T(8,128)(2,1)}, f32[2,3,1024]{2,1,0:T(4,128)}, bf16[2,1024,3,64]{1,3,2,0:T(8,128)(2,1)S(1)}, bf16[2,1024,...) while((s32[]{:T(128)}, bf16[2,1024,3,64]{1,3,2,0:T(8,128)(2,1)}, ...), condition=%wide.region_7.8_spmd.clone, body=%wide.region_2.7_spmd.sunk.clone | while | flops 834404352 | bytes 47524568 | solution.py:70
  115.9 30.3 %reduce-scatter.5.cloned.1.call-done = bf16[512,768]{1,0:T(8,128)(2,1)} async-done(((bf16[2048,768]{1,0:T(8,128)(2,1)}), bf16[512,768]{1,0:T(8,128)(2,1)}) %reduce-scatter.5.cloned.1.call-update) | async-done | bytes 786448 | tf_op jit(solution)/shard_map/reduce_scatter | solution.py:150
  150.8 28.2 %all-gather.8.cloned.1.call-done = bf16[2048,768]{1,0:T(8,128)(2,1)} async-done(((bf16[512,768]{1,0:T(8,128)(2,1)}), bf16[2048,768]{1,0:T(8,128)(2,1)}) %all-gather.8.cloned.1.call-update) | async-done | bytes 3145744 | tf_op jit(solution)/shard_map/all_gather | solution.py:163
  195.8 34.3 %reduce-scatter.7.cloned.1.call-done = bf16[512,768]{1,0:T(8,128)(2,1)} async-done(((bf16[2048,768]{1,0:T(8,128)(2,1)}), bf16[512,768]{1,0:T(8,128)(2,1)}) %reduce-scatter.7.cloned.1.call-update) | async-done | bytes 786448 | tf_op jit(solution)/shard_map/reduce_scatter | solution.py:167
  234.3 28.6 %all-gather.10.cloned.1.call-done = bf16[2048,768]{1,0:T(8,128)(2,1)} async-done(((bf16[512,768]{1,0:T(8,128)(2,1)}), bf16[2048,768]{1,0:T(8,128)(2,1)}) %all-gather.10.cloned.1.call-update) | async-done | bytes 3145744 | tf_op jit(solution)/shard_map/all_gather | solution.py:265
  262.9 10.9 %fusion.215 = (bf16[768]{0:T(1024)(128)(2,1)}, bf16[2048,768]{1,0:T(8,128)(2,1)S(1)}) fusion(f32[2048,768]{1,0:T(8,128)} %copy-done.93, f32[768]{0:T(1024)} %param.30, bf16[2048,768]{1,0:T(8,128)(2,1)} %all-gather.10.cloned.1.call-done, bf16[768,768]{1,0:T(8,128)(2,1)S(1)} %copy-done), kind=kOutput, calls=%fused_computation.265 | convolution fusion | flops 2450521344 | bytes 13767168 | tf_op jit(solution)/shard_map/td,fd->tf/dot_general | solution.py:267
  279.6 38.1 %reduce-scatter.9.cloned.1.call-done = bf16[512,768]{1,0:T(8,128)(2,1)} async-done(((bf16[2048,768]{1,0:T(8,128)(2,1)}), bf16[512,768]{1,0:T(8,128)(2,1)}) %reduce-scatter.9.cloned.1.call-update) | async-done | bytes 786448 | tf_op jit(solution)/shard_map/reduce_scatter | solution.py:274
  338.7 13.8 %all-gather.12.cloned.1.call-done = bf16[2048,768]{1,0:T(8,128)(2,1)} async-done(((bf16[512,768]{1,0:T(8,128)(2,1)}), bf16[2048,768]{1,0:T(8,128)(2,1)}) %all-gather.12.cloned.1.call-update) | async-done | bytes 3145744 | tf_op jit(solution)/shard_map/all_gather | solution.py:290
  360.3 149.5 %while.29 = (s32[]{:T(128)}, f32[2,1024,3,64]{1,3,2,0:T(8,128)}, f32[2,1024,3,64]{1,3,2,0:T(8,128)}, bf16[2,1024,3,64]{1,3,2,0:T(8,128)(2,1)}, bf16[2,1024,3,64]...) while((s32[]{:T(128)}, f32[2,1024,3,64]{1,3,2,0:T(8,128)}, ...), condition=%wide.region_18.19_spmd.clone, body=%wide.region_15.18_spmd.sunk.clone | while | flops 2079926272 | bytes 209329936 | solution.py:107
  372.9 14.0 %fusion.347 = f32[512,3,64]{0,2,1:T(8,128)S(1)} fusion(f32[3,512,1024]{2,1,0:T(8,128)} %fusion.344, f32[3,512,1024]{2,1,0:T(8,128)} %copy-done.2, f32[3,512]{1,0:T(4,128)S(1)} %get-tuple-element.382, bf16[2,1024,3,64]{1,3,2,0:T(8,128)(2,1)S(1)} %get-tuple-element.436, s32[]{:T(128)S(6)} %copy.116), kind=kOutput, calls=%fused_computation.72.clone.1.clone | convolution fusion | flops 215484928 | bytes 25968644 | tf_op jit(solution)/shard_map/while/body/eval_jaxpr/hqk,khe->qhe/dot_general | solution.py:100
  391.5 14.2 %fusion.350 = f32[512,3,64]{0,2,1:T(8,128)S(1)} fusion(f32[3,512,1024]{2,1,0:T(8,128)} %fusion.348, f32[3,512,1024]{2,1,0:T(8,128)} %copy-done.3, f32[3,512]{1,0:T(4,128)S(1)} %get-tuple-element.383, bf16[2,1024,3,64]{1,3,2,0:T(8,128)(2,1)S(1)} %get-tuple-element.436, s32[]{:T(128)S(6)} %copy.116), kind=kOutput, calls=%fused_computation.73.clone.1.clone | convolution fusion | flops 215484928 | bytes 25968644 | tf_op jit(solution)/shard_map/while/body/eval_jaxpr/hqk,khe->qhe/dot_general | solution.py:100
  405.7 14.1 %fusion.352 = f32[3,64,1024]{2,1,0:T(8,128)} fusion(f32[3,512,1024]{2,1,0:T(8,128)} %fusion.348, f32[3,512,1024]{2,1,0:T(8,128)} %copy-done.3, f32[3,512]{1,0:T(4,128)S(1)} %get-tuple-element.383, bf16[2,1024,3,64]{1,3,2,0:T(8,128)(2,1)S(1)} %get-tuple-element.437, s32[]{:T(128)S(6)} %copy.116), kind=kOutput, calls=%fused_computation.47.clone.1.clone | convolution fusion | flops 215484928 | bytes 26165252 | tf_op jit(solution)/shard_map/while/body/eval_jaxpr/hqk,qhe->khe/dot_general | solution.py:102
  419.8 14.3 %fusion.353 = f32[2,1024,3,64]{1,3,2,0:T(8,128)} fusion(f32[2,1024,3,64]{1,3,2,0:T(8,128)} %get-tuple-element.425, s32[]{:T(128)S(6)} %copy.116, f32[3,64,1024]{2,1,0:T(8,128)} %fusion.352, f32[3,512,1024]{2,1,0:T(8,128)} %fusion.344, f32[3,512,1024]{2,1,0:T(8,128)} %copy-done.2, f32[3,512]{1,0:T(4,128)S(1)} %get-tuple-element.382, ...), kind=kOutput, calls=%fused_computation.71.clone.1.clone | convolution fusion | flops 215681536 | bytes 26953216 | tf_op jit(solution)/shard_map/while/body/eval_jaxpr/hqk,qhe->khe/dot_general | solution.py:102
  447.3 14.0 %fusion.347 = f32[512,3,64]{0,2,1:T(8,128)S(1)} fusion(f32[3,512,1024]{2,1,0:T(8,128)} %fusion.344, f32[3,512,1024]{2,1,0:T(8,128)} %copy-done.2, f32[3,512]{1,0:T(4,128)S(1)} %get-tuple-element.382, bf16[2,1024,3,64]{1,3,2,0:T(8,128)(2,1)S(1)} %get-tuple-element.436, s32[]{:T(128)S(6)} %copy.116), kind=kOutput, calls=%fused_computation.72.clone.1.clone | convolution fusion | flops 215484928 | bytes 25968644 | tf_op jit(solution)/shard_map/while/body/eval_jaxpr/hqk,khe->qhe/dot_general | solution.py:100
  465.9 14.2 %fusion.350 = f32[512,3,64]{0,2,1:T(8,128)S(1)} fusion(f32[3,512,1024]{2,1,0:T(8,128)} %fusion.348, f32[3,512,1024]{2,1,0:T(8,128)} %copy-done.3, f32[3,512]{1,0:T(4,128)S(1)} %get-tuple-element.383, bf16[2,1024,3,64]{1,3,2,0:T(8,128)(2,1)S(1)} %get-tuple-element.436, s32[]{:T(128)S(6)} %copy.116), kind=kOutput, calls=%fused_computation.73.clone.1.clone | convolution fusion | flops 215484928 | bytes 25968644 | tf_op jit(solution)/shard_map/while/body/eval_jaxpr/hqk,khe->qhe/dot_general | solution.py:100
  480.1 14.1 %fusion.352 = f32[3,64,1024]{2,1,0:T(8,128)} fusion(f32[3,512,1024]{2,1,0:T(8,128)} %fusion.348, f32[3,512,1024]{2,1,0:T(8,128)} %copy-done.3, f32[3,512]{1,0:T(4,128)S(1)} %get-tuple-element.383, bf16[2,1024,3,64]{1,3,2,0:T(8,128)(2,1)S(1)} %get-tuple-element.437, s32[]{:T(128)S(6)} %copy.116), kind=kOutput, calls=%fused_computation.47.clone.1.clone | convolution fusion | flops 215484928 | bytes 26165252 | tf_op jit(solution)/shard_map/while/body/eval_jaxpr/hqk,qhe->khe/dot_general | solution.py:102
  494.2 14.3 %fusion.353 = f32[2,1024,3,64]{1,3,2,0:T(8,128)} fusion(f32[2,1024,3,64]{1,3,2,0:T(8,128)} %get-tuple-element.425, s32[]{:T(128)S(6)} %copy.116, f32[3,64,1024]{2,1,0:T(8,128)} %fusion.352, f32[3,512,1024]{2,1,0:T(8,128)} %fusion.344, f32[3,512,1024]{2,1,0:T(8,128)} %copy-done.2, f32[3,512]{1,0:T(4,128)S(1)} %get-tuple-element.382, ...), kind=kOutput, calls=%fused_computation.71.clone.1.clone | convolution fusion | flops 215681536 | bytes 26953216 | tf_op jit(solution)/shard_map/while/body/eval_jaxpr/hqk,qhe->khe/dot_general | solution.py:102
  535.2 13.0 %all-reduce.4 = s32[16]{0:T(128)S(1)} all-reduce(s32[16]{0:T(128)S(1)} %dynamic-update-slice), channel_id=1, replica_groups=mesh['wide'=8,'narrow'=4] {'wide'}, use_global_device_ids=true, to_apply=%add.4 | all-reduce | flops 16 | bytes 128
  548.5 119.4 %all-reduce.10.cloned.1.call-done = (bf16[3,768,192]{1,2,0:T(8,128)(2,1)}, bf16[192,768]{1,0:T(8,128)(2,1)}, bf16[768,768]{1,0:T(8,128)(2,1)}, bf16[768,768]{1,0:T(8,128)(2,1)}) async-done(((bf16[3,768,192]{1,2,0:T(8,128)(2,1)}, bf16[192,768]{1,0:T(8,128)(2,1)}, bf16[768,768]{1,0:T(8,128)(2,1)}, bf16[768,768]{1,0:T(8,128)(2,1)}), (bf16[3,768,192]{1,2,0:T(8,128)(2,1)}, bf16[192,768]{1,0:T(8,128)(2,1)}, ...) | async-done | bytes 3538960 | tf_op jit(solution)/shard_map/psum | solution.py:357
  675.6 31.7 %reduce-scatter.11.cloned.1.call-done = bf16[512,768]{1,0:T(8,128)(2,1)} async-done(((bf16[2048,768]{1,0:T(8,128)(2,1)}), bf16[512,768]{1,0:T(8,128)(2,1)}) %reduce-scatter.11.cloned.1.call-update) | async-done | bytes 786448 | tf_op jit(solution)/shard_map/reduce_scatter | solution.py:306
  739.6 11.6 %all-reduce.7 = (bf16[2,4608]{1,0:T(2,128)(2,1)}, bf16[768]{0:T(1024)(128)(2,1)}, bf16[768]{0:T(1024)(128)(2,1)}, bf16[768]{0:T(1024)(128)(2,1)}) all-reduce(bf16[2,4608]{1,0:T(2,128)(2,1)} %convolution_convert_fusion, bf16[768]{0:T(1024)(128)(2,1)} %get-tuple-element.147, ...), channel_id=1, replica_groups=mesh['wide'=8,'narrow'=4] {'narrow'}, use_global_device_ids=true, to_apply=%region_22.23 | all-reduce | flops 11520 | bytes 46080 | tf_op jit(solution)/shard_map/psum | solution.py:331
  751.2 22.5 %all-reduce.5 = (bf16[768]{0:T(1024)(128)(2,1)}, bf16[768]{0:T(1024)(128)(2,1)}, bf16[768]{0:T(1024)(128)(2,1)}, bf16[768]{0:T(1024)(128)(2,1)}) all-reduce(bf16[768]{0:T(1024)(128)(2,1)} %get-tuple-element.188, bf16[768]{0:T(1024)(128)(2,1)} %get-tuple-element.189, ...), channel_id=1, replica_groups=mesh['wide'=8,'narrow'=4] {'wide'}, use_global_device_ids=true, to_apply=%region_26.27 | all-reduce | flops 3072 | bytes 12288 | tf_op jit(solution)/shard_map/psum | solution.py:357
  779.5 30.9 %all-gather = f32[8,2,4608]{2,1,0:T(2,128)S(1)} all-gather(f32[1,2,4608]{2,1,0:T(2,128)S(1)} %bitcast_convert_fusion.1), channel_id=1, replica_groups=mesh['wide'=8,'narrow'=4] {'wide'}, dimensions={0}, use_global_device_ids=true | all-gather | bytes 331776 | tf_op jit(solution)/shard_map/all_gather | solution.py:336
  (365 shorter events, 257.9 us)
Async XLA Ops:
  7.2 179.4 %copy-start = (bf16[768,768]{1,0:T(8,128)(2,1)S(1)}, bf16[768,768]{1,0:T(8,128)(2,1)}, u32[]{:S(2)}) copy-start(bf16[768,768]{1,0:T(8,128)(2,1)} %param.31) | copy-start | bytes 3538948
  7.2 53.5 %all-gather.6.cloned.1.call-start = ((), (), s32[]{:S(2)}) async-start(), calls=%async_computation.4 | async-start | bytes 3932160 | tf_op jit(solution)/shard_map/all_gather | solution.py:141
  29.3 116.8 %reduce-scatter.5.cloned.1.call-start = ((), (), s32[]{:S(2)}) async-start(), calls=%async_computation.5 | async-start | bytes 3932160 | tf_op jit(solution)/shard_map/reduce_scatter | solution.py:150
  108.0 71.0 %all-gather.8.cloned.1.call-start = ((), (), s32[]{:S(2)}) async-start(), calls=%async_computation.6 | async-start | bytes 3932160 | tf_op jit(solution)/shard_map/all_gather | solution.py:163
  148.5 172.2 %copy-start.4 = (f32[512,768]{1,0:T(8,128)}, f32[512,768]{1,0:T(8,128)S(1)}, u32[]{:S(2)}) copy-start(f32[512,768]{1,0:T(8,128)S(1)} %get-tuple-element.198) | copy-start | bytes 4718596
  148.5 172.2 %copy-start.62 = (f32[512]{0:T(512)}, f32[512]{0:T(512)S(1)}, u32[]{:S(2)}) copy-start(f32[512]{0:T(512)S(1)} %broadcast_multiply_fusion.2) | copy-start | bytes 6148
  149.0 171.7 %copy-start.72 = (f32[512]{0:T(512)}, f32[512]{0:T(512)S(1)}, u32[]{:S(2)}) copy-start(f32[512]{0:T(512)S(1)} %fusion.207) | copy-start | bytes 6148
  150.3 79.8 %reduce-scatter.7.cloned.1.call-start = ((), (), s32[]{:S(2)}) async-start(), calls=%async_computation.7 | async-start | bytes 3932160 | tf_op jit(solution)/shard_map/reduce_scatter | solution.py:167
  150.8 35.8 %copy-start.89 = (f32[768]{0:T(1024)S(1)}, f32[768]{0:T(1024)}, u32[]{:S(2)}) copy-start(f32[768]{0:T(1024)} %param.30) | copy-start | bytes 9220
  192.0 70.9 %all-gather.10.cloned.1.call-start = ((), (), s32[]{:S(2)}) async-start(), calls=%async_computation.8 | async-start | bytes 3932160 | tf_op jit(solution)/shard_map/all_gather | solution.py:265
  192.8 128.7 %copy-start.64 = (f32[512]{0:T(512)}, f32[512]{0:T(512)S(1)}, u32[]{:S(2)}) copy-start(f32[512]{0:T(512)S(1)} %convert_element_type.178) | copy-start | bytes 6148
  234.2 83.4 %reduce-scatter.9.cloned.1.call-start = ((), (), s32[]{:S(2)}) async-start(), calls=%async_computation.9 | async-start | bytes 3932160 | tf_op jit(solution)/shard_map/reduce_scatter | solution.py:274
  279.5 41.1 %copy-start.80 = (f32[512]{0:T(512)S(1)}, f32[512]{0:T(512)}, u32[]{:S(2)}) copy-start(f32[512]{0:T(512)} %copy-done.79) | copy-start | bytes 6148
  279.5 73.1 %all-gather.12.cloned.1.call-start = ((), (), s32[]{:S(2)}) async-start(), calls=%async_computation.10 | async-start | bytes 3932160 | tf_op jit(solution)/shard_map/all_gather | solution.py:290
  323.9 344.0 %all-reduce.10.cloned.1.call-start = ((), (), s32[]{:S(2)}) async-start(), calls=%async_computation.12 | async-start | bytes 7077888 | tf_op jit(solution)/shard_map/psum | solution.py:357
  527.1 180.2 %reduce-scatter.11.cloned.1.call-start = ((), (), s32[]{:S(2)}) async-start(), calls=%async_computation.11 | async-start | bytes 3932160 | tf_op jit(solution)/shard_map/reduce_scatter | solution.py:306
  548.2 124.2 %copy-start.82 = (s32[16]{0:T(128)}, s32[16]{0:T(128)S(1)}, u32[]{:S(2)}) copy-start(s32[16]{0:T(128)S(1)} %all-reduce.4) | copy-start | bytes 196
  672.4 34.9 %copy-start.7 = (bf16[512,768]{1,0:T(8,128)(2,1)S(1)}, bf16[512,768]{1,0:T(8,128)(2,1)}, u32[]{:S(2)}) copy-start(bf16[512,768]{1,0:T(8,128)(2,1)} %param.19) | copy-start | bytes 2359300
  672.4 34.9 %copy-start.14 = (f32[512,1,768]{2,0,1:T(8,128)S(1)}, f32[512,1,768]{2,0,1:T(8,128)}, u32[]{:S(2)}) copy-start(f32[512,1,768]{2,0,1:T(8,128)} %copy-done.13) | copy-start | bytes 4718596
  672.4 34.9 %copy-start.61 = (f32[512]{0:T(512)S(1)}, f32[512]{0:T(512)}, u32[]{:S(2)}) copy-start(f32[512]{0:T(512)} %copy-done.60) | copy-start | bytes 6148
  672.4 34.9 %copy-start.67 = (f32[768]{0:T(1024)S(1)}, f32[768]{0:T(1024)}, u32[]{:S(2)}) copy-start(f32[768]{0:T(1024)} %param.25) | copy-start | bytes 9220
  674.0 35.8 %copy-start.78 = (f32[512]{0:T(512)S(1)}, f32[512]{0:T(512)}, u32[]{:S(2)}) copy-start(f32[512]{0:T(512)} %copy-done.77) | copy-start | bytes 6148
  730.8 82.6 %copy-start.38 = (bf16[128,4608]{1,0:T(8,128)(2,1)S(1)}, bf16[128,4608]{1,0:T(8,128)(2,1)}, u32[]{:S(2)}) copy-start(bf16[128,4608]{1,0:T(8,128)(2,1)} %param.23) | copy-start | bytes 3538948
  739.6 80.2 %copy-start.76 = (f32[512]{0:T(512)S(1)}, f32[512]{0:T(512)}, u32[]{:S(2)}) copy-start(f32[512]{0:T(512)} %copy-done.74) | copy-start | bytes 6148
  (88 other events, 448.2 us)
Sparse Core Ops, SparseCore 0:
  29.4 31.2 all-gather.5
  108.1 37.9 reduce-scatter.4
  150.4 28.5 all-gather.7
  192.2 37.9 reduce-scatter.6
  234.3 28.5 all-gather.9
  279.6 37.9 reduce-scatter.8
  324.0 28.5 all-gather.11
  527.3 140.5 all-reduce.9
  670.4 36.8 reduce-scatter.10
where the time goes:
time: 836 us; the launch traced here: 829 us
  waiting for transfers between devices  352 us (42%)
  matrix products  232 us (28%)
  local copies, waits for them, and re-layouts  85.4 us (10%)
  blocking collectives  77.9 us (9%)
  other arithmetic  63.3 us (8%)
  between operations  15.6 us (2%)
    psum x1, waiting for transfers between devices, reduce_low(): return lax.psum(values.astype(jnp.bfloat16), 'wide').astype(jnp.float32)  119 us
    dot_general x4, matrix products, one_sequence(): jnp.einsum('hqk,qhe->khe', grad_scores, q_block, preferred_element_type=j...  56.7 us
    dot_general x4, matrix products, one_sequence(): jnp.einsum('hqk,khe->qhe', grad_scores, k_seq, preferred_element_type=jnp...  56.3 us
    reduce_scatter x1, waiting for transfers between devices, body(): lax.psum_scatter(jnp.einsum('tf,df->td', lax.slice_in_dim(grad_pre_low, 0...  38.1 us
    reduce_scatter x1, waiting for transfers between devices, forward(): lax.psum_scatter(jnp.dot(lax.slice_in_dim(act_low, 0, tok_rows * lax.axis...  34.3 us
    unnamed x183, local copies, waits for them, and re-layouts  33.3 us
    reduce_scatter x1, waiting for transfers between devices, body(): lax.psum_scatter(jnp.einsum('kte,kde->td', grad_projected, w_qkv, preferr...  31.7 us
    all_gather x1, blocking collectives, body(): all_modulation = lax.all_gather(grad_modulation, 'wide', axis=0, tiled=True)  30.9 us
  transfers between devices with their start and end apart: 9, of which 9 were waited for; matrix products, arithmetic and copies ran while one was open for 5% of the time, Pallas kernels for 0%

commit v1 on v0

--- a/solution.py
+++ b/solution.py
@@ -333,7 +333,13 @@
         lax.psum(gain_two_part.astype(jnp.bfloat16), "narrow").astype(jnp.float32),
         lax.psum(b_down_part.astype(jnp.bfloat16), "narrow").astype(jnp.float32),
     )
-    all_modulation = lax.all_gather(grad_modulation, "wide", axis=0, tiled=True)
+    peers = lax.axis_size("wide")
+    held, blocks = (grad_modulation, [grad_modulation])
+    for _ in range(peers - 1):
+        held = lax.ppermute(held, "wide", [(i, (i + 1) % peers) for i in range(peers)])
+        blocks.insert(0, held)
+    line = jnp.concatenate(blocks, axis=0)
+    all_modulation = jnp.roll(line, (lax.axis_index("wide") + 1) * grad_modulation.shape[0], axis=0)
     all_steps = lax.all_gather(timestep, "wide", axis=0, tiled=True)
     all_pick = (
         all_steps[:, None] == jnp.arange(time_table.shape[0], dtype=jnp.int32)[None, :]

time: 836 us -> 786 us (0.940)
  blocking collectives: 77.9 us -> 45.4 us
  waiting for transfers between devices: 352 us -> 338 us
    psum x1, waiting for transfers between devices: 119 us -> 79.9 us  [reduce_low(): return lax.psum(values.astype(jnp.bfloat16), 'wide').astype(jnp.float32)]
    all_gather x1 -> x0, blocking collectives: 30.9 us -> none  [body(): all_modulation = lax.all_gather(grad_modulation, 'wide', axis=0, tiled=True)]
    ppermute x0 -> x7, waiting for transfers between devices: none -> 23.6 us  [body(): lax.ppermute(held, 'wide', [(i, (i + 1) % peers) for i in range(peers)])]
    all_gather x1, waiting for transfers between devices: 13.8 us -> 28.6 us  [body(): lax.all_gather((grad_mid * mod_tok[:, 2]).astype(jnp.bfloat16), 'narrow',...]
    reduce_scatter x1, waiting for transfers between devices: 31.7 us -> 18.2 us  [body(): lax.psum_scatter(jnp.einsum('kte,kde->td', grad_projected, w_qkv, preferr...]
    unnamed x183 -> x207, local copies, waits for them, and re-layouts: 33.3 us -> 30.4 us
  transfers between devices with their start and end apart: 9 -> 16, of which waited for: 9 -> 13; matrix products, arithmetic and copies ran while one was open for 5% -> 10% of each run, Pallas kernels for 0% -> 0%
where the time goes in v1:
time: 786 us; the launch traced here: 779 us
  waiting for transfers between devices  338 us (43%)
  matrix products  230 us (29%)
  local copies, waits for them, and re-layouts  83.8 us (11%)
  other arithmetic  58.6 us (7%)
  blocking collectives  45.4 us (6%)
  between operations  15.7 us (2%)
    psum x1, waiting for transfers between devices, reduce_low(): return lax.psum(values.astype(jnp.bfloat16), 'wide').astype(jnp.float32)  79.9 us
    dot_general x4, matrix products, one_sequence(): jnp.einsum('hqk,qhe->khe', grad_scores, q_block, preferred_element_type=j...  57.5 us
    dot_general x4, matrix products, one_sequence(): jnp.einsum('hqk,khe->qhe', grad_scores, k_seq, preferred_element_type=jnp...  55.8 us
    reduce_scatter x1, waiting for transfers between devices, body(): lax.psum_scatter(jnp.einsum('tf,df->td', lax.slice_in_dim(grad_pre_low, 0...  38.1 us
    reduce_scatter x1, waiting for transfers between devices, forward(): lax.psum_scatter(jnp.dot(lax.slice_in_dim(act_low, 0, tok_rows * lax.axis...  34.3 us
    unnamed x207, local copies, waits for them, and re-layouts  30.4 us
    reduce_scatter x1, waiting for transfers between devices, forward(): lax.psum_scatter(jnp.dot(lax.slice_in_dim(heads_low, 0, tok_rows * lax.ax...  30.3 us
    all_gather x1, waiting for transfers between devices, body(): lax.all_gather(grad_branch.astype(jnp.bfloat16), 'narrow', axis=0, tiled=...  28.6 us
  transfers between devices with their start and end apart: 16, of which 13 were waited for; matrix products, arithmetic and copies ran while one was open for 10% of the time, Pallas kernels for 0%

profile of v1, /device:TPU:0, one launch (start us, length us, event | category | flops | bytes accessed | tf_op | source)
XLA Modules:
  0.0 779.1 jit_solution(2683376683679497840)
XLA Ops:
  32.8 27.9 %all-gather.5.cloned.1.call-done = bf16[2048,768]{1,0:T(8,128)(2,1)} async-done(((bf16[512,768]{1,0:T(8,128)(2,1)}), bf16[2048,768]{1,0:T(8,128)(2,1)}) %all-gather.5.cloned.1.call-update) | async-done | bytes 3145744 | tf_op jit(solution)/shard_map/all_gather | solution.py:141
  81.2 20.5 %while.28 = (s32[]{:T(128)}, bf16[2,1024,3,64]{1,3,2,0:T(8,128)(2,1)}, f32[2,3,1024]{2,1,0:T(4,128)}, bf16[2,1024,3,64]{1,3,2,0:T(8,128)(2,1)S(1)}, bf16[2,1024,...) while((s32[]{:T(128)}, bf16[2,1024,3,64]{1,3,2,0:T(8,128)(2,1)}, ...), condition=%wide.region_7.8_spmd.clone, body=%wide.region_2.7_spmd.sunk.clone | while | flops 834404352 | bytes 47524568 | solution.py:70
  115.9 30.3 %reduce-scatter.5.cloned.1.call-done = bf16[512,768]{1,0:T(8,128)(2,1)} async-done(((bf16[2048,768]{1,0:T(8,128)(2,1)}), bf16[512,768]{1,0:T(8,128)(2,1)}) %reduce-scatter.5.cloned.1.call-update) | async-done | bytes 786448 | tf_op jit(solution)/shard_map/reduce_scatter | solution.py:150
  150.9 28.2 %all-gather.7.cloned.1.call-done = bf16[2048,768]{1,0:T(8,128)(2,1)} async-done(((bf16[512,768]{1,0:T(8,128)(2,1)}), bf16[2048,768]{1,0:T(8,128)(2,1)}) %all-gather.7.cloned.1.call-update) | async-done | bytes 3145744 | tf_op jit(solution)/shard_map/all_gather | solution.py:163
  195.7 34.3 %reduce-scatter.7.cloned.1.call-done = bf16[512,768]{1,0:T(8,128)(2,1)} async-done(((bf16[2048,768]{1,0:T(8,128)(2,1)}), bf16[512,768]{1,0:T(8,128)(2,1)}) %reduce-scatter.7.cloned.1.call-update) | async-done | bytes 786448 | tf_op jit(solution)/shard_map/reduce_scatter | solution.py:167
  234.2 28.6 %all-gather.9.cloned.1.call-done = bf16[2048,768]{1,0:T(8,128)(2,1)} async-done(((bf16[512,768]{1,0:T(8,128)(2,1)}), bf16[2048,768]{1,0:T(8,128)(2,1)}) %all-gather.9.cloned.1.call-update) | async-done | bytes 3145744 | tf_op jit(solution)/shard_map/all_gather | solution.py:265
  262.8 10.9 %fusion.218 = (bf16[768]{0:T(1024)(128)(2,1)}, bf16[2048,768]{1,0:T(8,128)(2,1)S(1)}) fusion(f32[2048,768]{1,0:T(8,128)} %copy-done.105, f32[768]{0:T(1024)} %param.30, bf16[2048,768]{1,0:T(8,128)(2,1)} %all-gather.9.cloned.1.call-done, bf16[768,768]{1,0:T(8,128)(2,1)S(1)} %copy-done), kind=kOutput, calls=%fused_computation.269 | convolution fusion | flops 2450521344 | bytes 13767168 | tf_op jit(solution)/shard_map/td,fd->tf/dot_general | solution.py:267
  279.5 38.1 %reduce-scatter.9.cloned.1.call-done = bf16[512,768]{1,0:T(8,128)(2,1)} async-done(((bf16[2048,768]{1,0:T(8,128)(2,1)}), bf16[512,768]{1,0:T(8,128)(2,1)}) %reduce-scatter.9.cloned.1.call-update) | async-done | bytes 786448 | tf_op jit(solution)/shard_map/reduce_scatter | solution.py:274
  323.9 28.6 %all-gather.11.cloned.1.call-done = bf16[2048,768]{1,0:T(8,128)(2,1)} async-done(((bf16[512,768]{1,0:T(8,128)(2,1)}), bf16[2048,768]{1,0:T(8,128)(2,1)}) %all-gather.11.cloned.1.call-update) | async-done | bytes 3145744 | tf_op jit(solution)/shard_map/all_gather | solution.py:290
  360.2 149.6 %while.29 = (s32[]{:T(128)}, f32[2,1024,3,64]{1,3,2,0:T(8,128)}, f32[2,1024,3,64]{1,3,2,0:T(8,128)}, bf16[2,1024,3,64]{1,3,2,0:T(8,128)(2,1)}, bf16[2,1024,3,64]...) while((s32[]{:T(128)}, f32[2,1024,3,64]{1,3,2,0:T(8,128)}, ...), condition=%wide.region_18.19_spmd.clone, body=%wide.region_15.18_spmd.sunk.clone | while | flops 2079926272 | bytes 209329936 | solution.py:107
  372.8 14.2 %fusion.346 = f32[512,3,64]{0,2,1:T(8,128)S(1)} fusion(f32[3,512,1024]{2,1,0:T(8,128)} %fusion.343, f32[3,512,1024]{2,1,0:T(8,128)} %copy-done.2, f32[3,512]{1,0:T(4,128)S(1)} %get-tuple-element.365, bf16[2,1024,3,64]{1,3,2,0:T(8,128)(2,1)S(1)} %get-tuple-element.419, s32[]{:T(128)S(6)} %copy.95), kind=kOutput, calls=%fused_computation.72.clone.1.clone | convolution fusion | flops 215484928 | bytes 25968644 | tf_op jit(solution)/shard_map/while/body/eval_jaxpr/hqk,khe->qhe/dot_general | solution.py:100
  391.7 13.7 %fusion.349 = f32[512,3,64]{0,2,1:T(8,128)S(1)} fusion(f32[3,512,1024]{2,1,0:T(8,128)} %fusion.347, f32[3,512,1024]{2,1,0:T(8,128)} %copy-done.3, f32[3,512]{1,0:T(4,128)S(1)} %get-tuple-element.366, bf16[2,1024,3,64]{1,3,2,0:T(8,128)(2,1)S(1)} %get-tuple-element.419, s32[]{:T(128)S(6)} %copy.95), kind=kOutput, calls=%fused_computation.73.clone.1.clone | convolution fusion | flops 215484928 | bytes 25968644 | tf_op jit(solution)/shard_map/while/body/eval_jaxpr/hqk,khe->qhe/dot_general | solution.py:100
  405.3 14.1 %fusion.351 = f32[3,64,1024]{2,1,0:T(8,128)} fusion(f32[3,512,1024]{2,1,0:T(8,128)} %fusion.347, f32[3,512,1024]{2,1,0:T(8,128)} %copy-done.3, f32[3,512]{1,0:T(4,128)S(1)} %get-tuple-element.366, bf16[2,1024,3,64]{1,3,2,0:T(8,128)(2,1)S(1)} %get-tuple-element.420, s32[]{:T(128)S(6)} %copy.95), kind=kOutput, calls=%fused_computation.47.clone.1.clone | convolution fusion | flops 215484928 | bytes 26165252 | tf_op jit(solution)/shard_map/while/body/eval_jaxpr/hqk,qhe->khe/dot_general | solution.py:102
  419.4 14.7 %fusion.352 = f32[2,1024,3,64]{1,3,2,0:T(8,128)} fusion(f32[2,1024,3,64]{1,3,2,0:T(8,128)} %get-tuple-element.408, s32[]{:T(128)S(6)} %copy.95, f32[3,64,1024]{2,1,0:T(8,128)} %fusion.351, f32[3,512,1024]{2,1,0:T(8,128)} %fusion.343, f32[3,512,1024]{2,1,0:T(8,128)} %copy-done.2, f32[3,512]{1,0:T(4,128)S(1)} %get-tuple-element.365, ...), kind=kOutput, calls=%fused_computation.71.clone.1.clone | convolution fusion | flops 215681536 | bytes 26953216 | tf_op jit(solution)/shard_map/while/body/eval_jaxpr/hqk,qhe->khe/dot_general | solution.py:102
  447.4 14.2 %fusion.346 = f32[512,3,64]{0,2,1:T(8,128)S(1)} fusion(f32[3,512,1024]{2,1,0:T(8,128)} %fusion.343, f32[3,512,1024]{2,1,0:T(8,128)} %copy-done.2, f32[3,512]{1,0:T(4,128)S(1)} %get-tuple-element.365, bf16[2,1024,3,64]{1,3,2,0:T(8,128)(2,1)S(1)} %get-tuple-element.419, s32[]{:T(128)S(6)} %copy.95), kind=kOutput, calls=%fused_computation.72.clone.1.clone | convolution fusion | flops 215484928 | bytes 25968644 | tf_op jit(solution)/shard_map/while/body/eval_jaxpr/hqk,khe->qhe/dot_general | solution.py:100
  466.3 13.7 %fusion.349 = f32[512,3,64]{0,2,1:T(8,128)S(1)} fusion(f32[3,512,1024]{2,1,0:T(8,128)} %fusion.347, f32[3,512,1024]{2,1,0:T(8,128)} %copy-done.3, f32[3,512]{1,0:T(4,128)S(1)} %get-tuple-element.366, bf16[2,1024,3,64]{1,3,2,0:T(8,128)(2,1)S(1)} %get-tuple-element.419, s32[]{:T(128)S(6)} %copy.95), kind=kOutput, calls=%fused_computation.73.clone.1.clone | convolution fusion | flops 215484928 | bytes 25968644 | tf_op jit(solution)/shard_map/while/body/eval_jaxpr/hqk,khe->qhe/dot_general | solution.py:100
  479.9 14.1 %fusion.351 = f32[3,64,1024]{2,1,0:T(8,128)} fusion(f32[3,512,1024]{2,1,0:T(8,128)} %fusion.347, f32[3,512,1024]{2,1,0:T(8,128)} %copy-done.3, f32[3,512]{1,0:T(4,128)S(1)} %get-tuple-element.366, bf16[2,1024,3,64]{1,3,2,0:T(8,128)(2,1)S(1)} %get-tuple-element.420, s32[]{:T(128)S(6)} %copy.95), kind=kOutput, calls=%fused_computation.47.clone.1.clone | convolution fusion | flops 215484928 | bytes 26165252 | tf_op jit(solution)/shard_map/while/body/eval_jaxpr/hqk,qhe->khe/dot_general | solution.py:102
  494.0 14.7 %fusion.352 = f32[2,1024,3,64]{1,3,2,0:T(8,128)} fusion(f32[2,1024,3,64]{1,3,2,0:T(8,128)} %get-tuple-element.408, s32[]{:T(128)S(6)} %copy.95, f32[3,64,1024]{2,1,0:T(8,128)} %fusion.351, f32[3,512,1024]{2,1,0:T(8,128)} %fusion.343, f32[3,512,1024]{2,1,0:T(8,128)} %copy-done.2, f32[3,512]{1,0:T(4,128)S(1)} %get-tuple-element.365, ...), kind=kOutput, calls=%fused_computation.71.clone.1.clone | convolution fusion | flops 215681536 | bytes 26953216 | tf_op jit(solution)/shard_map/while/body/eval_jaxpr/hqk,qhe->khe/dot_general | solution.py:102
  545.1 18.2 %reduce-scatter.11.cloned.1.call-done = bf16[512,768]{1,0:T(8,128)(2,1)} async-done(((bf16[2048,768]{1,0:T(8,128)(2,1)}), bf16[512,768]{1,0:T(8,128)(2,1)}) %reduce-scatter.11.cloned.1.call-update) | async-done | bytes 786448 | tf_op jit(solution)/shard_map/reduce_scatter | solution.py:306
  574.4 9.9 %copy.66 = f32[512,6,768]{0,2,1:T(8,128)} copy(f32[512,6,768]{2,0,1:T(8,128)} %bitcast_dynamic-update-slice_fusion) | data formatting | bytes 18874368 | tf_op jit(solution)/shard_map/stack | solution.py:318
  594.5 12.0 %all-reduce.7 = (bf16[2,4608]{1,0:T(2,128)(2,1)S(1)}, bf16[768]{0:T(1024)(128)(2,1)}, bf16[768]{0:T(1024)(128)(2,1)}, bf16[768]{0:T(1024)(128)(2,1)}) all-reduce(bf16[2,4608]{1,0:T(2,128)(2,1)S(1)} %convolution_convert_fusion, bf16[768]{0:T(1024)(128)(2,1)S(1)} %get-tuple-element.132, ...), channel_id=1, replica_groups=mesh['wide'=8,'narrow'=4] {'narrow'}, use_global_device_ids=true, to_apply=%region_22.23 | all-reduce | flops 11520 | bytes 46080 | tf_op jit(solution)/shard_map/psum | solution.py:331
  615.7 11.3 %all-reduce.4 = s32[16]{0:T(128)S(1)} all-reduce(s32[16]{0:T(128)S(1)} %dynamic-update-slice), channel_id=1, replica_groups=mesh['wide'=8,'narrow'=4] {'wide'}, use_global_device_ids=true, to_apply=%add.4 | all-reduce | flops 16 | bytes 128
  630.5 79.9 %all-reduce.10.cloned.1.call-done = (bf16[3,768,192]{1,2,0:T(8,128)(2,1)}, bf16[192,768]{1,0:T(8,128)(2,1)}, bf16[768,768]{1,0:T(8,128)(2,1)}, bf16[768,768]{1,0:T(8,128)(2,1)}) async-done(((bf16[3,768,192]{1,2,0:T(8,128)(2,1)}, bf16[192,768]{1,0:T(8,128)(2,1)}, bf16[768,768]{1,0:T(8,128)(2,1)}, bf16[768,768]{1,0:T(8,128)(2,1)}), (bf16[3,768,192]{1,2,0:T(8,128)(2,1)}, bf16[192,768]{1,0:T(8,128)(2,1)}, ...) | async-done | bytes 3538960 | tf_op jit(solution)/shard_map/psum | solution.py:363
  739.7 22.1 %all-reduce.5 = (bf16[768]{0:T(1024)(128)(2,1)S(1)}, bf16[768]{0:T(1024)(128)(2,1)S(1)}, bf16[768]{0:T(1024)(128)(2,1)S(1)}, bf16[768]{0:T(1024)(128)(2,1)S(1)}) all-reduce(bf16[768]{0:T(1024)(128)(2,1)S(1)} %copy-done.92, bf16[768]{0:T(1024)(128)(2,1)S(1)} %copy-done.93, ...), channel_id=1, replica_groups=mesh['wide'=8,'narrow'=4] {'wide'}, use_global_device_ids=true, to_apply=%region_26.27 | all-reduce | flops 3072 | bytes 12288 | tf_op jit(solution)/shard_map/psum | solution.py:363
  (402 shorter events, 268.9 us)
Async XLA Ops:
  7.2 179.4 %copy-start = (bf16[768,768]{1,0:T(8,128)(2,1)S(1)}, bf16[768,768]{1,0:T(8,128)(2,1)}, u32[]{:S(2)}) copy-start(bf16[768,768]{1,0:T(8,128)(2,1)} %param.31) | copy-start | bytes 3538948
  7.2 53.5 %all-gather.5.cloned.1.call-start = ((), (), s32[]{:S(2)}) async-start(), calls=%async_computation.4 | async-start | bytes 3932160 | tf_op jit(solution)/shard_map/all_gather | solution.py:141
  29.3 116.9 %reduce-scatter.5.cloned.1.call-start = ((), (), s32[]{:S(2)}) async-start(), calls=%async_computation.5 | async-start | bytes 3932160 | tf_op jit(solution)/shard_map/reduce_scatter | solution.py:150
  108.0 71.0 %all-gather.7.cloned.1.call-start = ((), (), s32[]{:S(2)}) async-start(), calls=%async_computation.6 | async-start | bytes 3932160 | tf_op jit(solution)/shard_map/all_gather | solution.py:163
  148.5 172.1 %copy-start.4 = (f32[512,768]{1,0:T(8,128)}, f32[512,768]{1,0:T(8,128)S(1)}, u32[]{:S(2)}) copy-start(f32[512,768]{1,0:T(8,128)S(1)} %get-tuple-element.183) | copy-start | bytes 4718596
  148.5 172.1 %copy-start.68 = (f32[512]{0:T(512)}, f32[512]{0:T(512)S(1)}, u32[]{:S(2)}) copy-start(f32[512]{0:T(512)S(1)} %broadcast_multiply_fusion.2) | copy-start | bytes 6148
  149.0 171.6 %copy-start.78 = (f32[512]{0:T(512)}, f32[512]{0:T(512)S(1)}, u32[]{:S(2)}) copy-start(f32[512]{0:T(512)S(1)} %fusion.208) | copy-start | bytes 6148
  150.3 79.7 %reduce-scatter.7.cloned.1.call-start = ((), (), s32[]{:S(2)}) async-start(), calls=%async_computation.7 | async-start | bytes 3932160 | tf_op jit(solution)/shard_map/reduce_scatter | solution.py:167
  191.9 70.9 %all-gather.9.cloned.1.call-start = ((), (), s32[]{:S(2)}) async-start(), calls=%async_computation.8 | async-start | bytes 3932160 | tf_op jit(solution)/shard_map/all_gather | solution.py:265
  192.7 128.7 %copy-start.70 = (f32[512]{0:T(512)}, f32[512]{0:T(512)S(1)}, u32[]{:S(2)}) copy-start(f32[512]{0:T(512)S(1)} %convert_element_type.178) | copy-start | bytes 6148
  234.1 83.4 %reduce-scatter.9.cloned.1.call-start = ((), (), s32[]{:S(2)}) async-start(), calls=%async_computation.9 | async-start | bytes 3932160 | tf_op jit(solution)/shard_map/reduce_scatter | solution.py:274
  279.4 73.1 %all-gather.11.cloned.1.call-start = ((), (), s32[]{:S(2)}) async-start(), calls=%async_computation.10 | async-start | bytes 3932160 | tf_op jit(solution)/shard_map/all_gather | solution.py:290
  323.8 239.5 %reduce-scatter.11.cloned.1.call-start = ((), (), s32[]{:S(2)}) async-start(), calls=%async_computation.11 | async-start | bytes 3932160 | tf_op jit(solution)/shard_map/reduce_scatter | solution.py:306
  525.2 185.2 %all-reduce.10.cloned.1.call-start = ((), (), s32[]{:S(2)}) async-start(), calls=%async_computation.12 | async-start | bytes 7077888 | tf_op jit(solution)/shard_map/psum | solution.py:363
  606.5 110.1 %copy-start.59 = (bf16[2,4608]{1,0:T(2,128)(2,1)}, bf16[2,4608]{1,0:T(2,128)(2,1)S(1)}, u32[]{:S(2)}) copy-start(bf16[2,4608]{1,0:T(2,128)(2,1)S(1)} %get-tuple-element.172) | copy-start | bytes 55300
  606.5 7.7 collective-permute-start
  614.2 102.3 %copy-start.60 = (f32[2,4608]{1,0:T(2,128)}, f32[2,4608]{1,0:T(2,128)S(1)}, u32[]{:S(2)}) copy-start(f32[2,4608]{1,0:T(2,128)S(1)} %collective-permute-done) | copy-start | bytes 110596
  614.2 12.8 %collective-permute-start.1 = (f32[2,4608]{1,0:T(2,128)S(1)}, f32[2,4608]{1,0:T(2,128)S(1)}, u32[]{:S(2)}, u32[]{:S(2)}) collective-permute-start(f32[2,4608]{1,0:T(2,128)S(1)} %collective-permute-done), channel_id=1, source_target_pairs={{0,4},{4,8},{8,12},{12,16},{16,20},{20,24},{24,28},{28,0},{1,5},{5... | collective-permute-start | bytes 110600 | tf_op jit(solution)/shard_map/ppermute | solution.py:339
  627.0 89.5 %copy-start.61 = (f32[2,4608]{1,0:T(2,128)}, f32[2,4608]{1,0:T(2,128)S(1)}, u32[]{:S(2)}) copy-start(f32[2,4608]{1,0:T(2,128)S(1)} %collective-permute-done.1) | copy-start | bytes 110596
  627.0 91.1 %collective-permute-start.2 = (f32[2,4608]{1,0:T(2,128)S(1)}, f32[2,4608]{1,0:T(2,128)S(1)}, u32[]{:S(2)}, u32[]{:S(2)}) collective-permute-start(f32[2,4608]{1,0:T(2,128)S(1)} %collective-permute-done.1), channel_id=1, source_target_pairs={{0,4},{4,8},{8,12},{12,16},{16,20},{20,24},{24,28},{28,0},{1,5},{5... | collective-permute-start | bytes 110600 | tf_op jit(solution)/shard_map/ppermute | solution.py:339
  718.1 6.7 collective-permute-start.3
  724.8 6.7 collective-permute-start.4
  731.4 6.7 collective-permute-start.5
  738.1 26.1 %collective-permute-start.6 = (f32[2,4608]{1,0:T(2,128)S(1)}, f32[2,4608]{1,0:T(2,128)}, u32[]{:S(2)}, u32[]{:S(2)}) collective-permute-start(f32[2,4608]{1,0:T(2,128)S(1)} %collective-permute-done.5), channel_id=1, source_target_pairs={{0,4},{4,8},{8,12},{12,16},{16,20},{20,24},{24,28},{28,0},{1,5},{5... | collective-permute-start | bytes 110600 | tf_op jit(solution)/shard_map/ppermute | solution.py:339
  (107 other events, 1089.5 us)
Sparse Core Ops, SparseCore 0:
  29.4 31.2 all-gather.4
  108.1 37.9 reduce-scatter.4
  150.5 28.5 all-gather.6
  192.1 37.9 reduce-scatter.6
  234.2 28.5 all-gather.8
  279.6 37.9 reduce-scatter.8
  323.9 28.5 all-gather.10
  525.3 37.9 reduce-scatter.10
  568.4 141.9 all-reduce.9
